TPU v7x, 128 devices: a whole 4x4x4 slice. The times are simulated.
128 devices in a mesh: section: 8 (over y, z_lo), dp: 16 (over x, z_hi, core).
Axes of the slice: x: 4, y: 4, z: 4 (z_hi: 2, z_lo: 2; z = z_hi * 2 + z_lo), core: 2. Of those that a mesh axis runs over, the one named last changes fastest.
Arguments:
- enter_a: bfloat16 [8, 2048, 7168], P('section', 'dp'), may hold values from -6 to 6
- enter_b: bfloat16 [8, 2048, 7168], P('section', 'dp'), may hold values from -6 to 6
- cotan_a: bfloat16 [8, 2048, 7168], P('section', 'dp'), may hold values from -6 to 6
- cotan_b: bfloat16 [8, 2048, 7168], P('section', 'dp'), may hold values from -6 to 6
- saved_a: bfloat16 [2, 8, 2048, 7168], P(None, 'section', 'dp'), may hold values from -6 to 6
- saved_b: bfloat16 [2, 8, 2048, 7168], P(None, 'section', 'dp'), may hold values from -6 to 6
- norm_gain: float32 [8, 7168], P('section'), may hold values from 0.1 to 1.9
- w_down: bfloat16 [8, 7168, 256], P('section', 'dp'), may hold values from -0.0625 to 0.0625
- latent_gain: float32 [8, 256], P('section'), may hold values from 0.1 to 1.9
- w_up: bfloat16 [8, 256, 7168], P('section', None, 'dp'), may hold values from -0.375 to 0.375
Outputs:
- out_a: bfloat16 [8, 2048, 7168], P('section', 'dp')
- out_b: bfloat16 [8, 2048, 7168], P('section', 'dp')
- back_a: bfloat16 [8, 2048, 7168], P('section', 'dp')
- back_b: bfloat16 [8, 2048, 7168], P('section', 'dp')
- grad_norm_gain: float32 [8, 7168], P('section', 'dp')
- grad_down: float32 [8, 7168, 256], P('section', 'dp')
- grad_latent_gain: float32 [8, 256], P('section', 'dp')
- grad_up: float32 [8, 256, 7168], P('section', None, 'dp')
All inputs are finite; a program needn't handle non-finite values.
Results may differ from a plain program's by a relative error of at most 0.035.
Values may be sent and summed in bfloat16 or wider, within the bound.
No kernel may reach another device: no remote copies, remote signals or barrier semaphores. Data moves between devices by JAX's collectives and lax.ppermute only.
A program may use at most 192 MiB of HBM per device.

v0:
```python
import jax
import jax.numpy as jnp
from jax import lax
from jax.sharding import PartitionSpec as P

TICKS = 2


def swapped(value, axis, distance):
    return lax.ppermute(value, axis, [(i, i ^ 1 << distance) for i in range(lax.axis_size(axis))])


def from_behind(block, axis, distance):
    devices = range(lax.axis_size(axis))
    route = [(i - distance, i) for i in devices if i - distance in devices]
    return lax.ppermute(block, axis, route)


def shortened(value):

    def short(part):
        return part.astype(jnp.bfloat16) if part.dtype == jnp.float32 else part

    return jax.tree.map(short, value)


def layer(x, norm_gain, w_down, latent_gain, w_up):
    xf = x.astype(jnp.float32)
    normed = (xf * lax.rsqrt(jnp.mean(xf * xf, axis=-1, keepdims=True) + 1e-06) * norm_gain).astype(
        jnp.bfloat16
    )
    latent = jnp.dot(normed, w_down, preferred_element_type=jnp.float32)
    scaled = (
        latent * lax.rsqrt(jnp.mean(latent * latent, axis=-1, keepdims=True) + 1e-06) * latent_gain
    ).astype(jnp.bfloat16)
    return (xf + jnp.dot(scaled, w_up, preferred_element_type=jnp.float32)).astype(jnp.bfloat16)


def layer_grads(x, cotangent, weights):
    _, pull = jax.vjp(layer, x, *weights)
    return pull(cotangent)


def body(
    enter_a, enter_b, cotan_a, cotan_b, saved_a, saved_b, norm_gain, w_down, latent_gain, w_up
):
    section_count = lax.axis_size("section")
    section_bits = section_count.bit_length() - 1
    moved = (norm_gain, w_down, latent_gain, w_up)
    for bit in range(section_bits):
        moved = (
            swapped(moved[0].astype(jnp.bfloat16), "section", bit).astype(jnp.float32),
            swapped(moved[1], "section", bit),
            swapped(moved[2].astype(jnp.bfloat16), "section", bit).astype(jnp.float32),
            swapped(moved[3], "section", bit),
        )
    mirror_small = tuple((v[0] for v in moved))
    full = (
        lax.all_gather(w_down[0], "dp", axis=0, tiled=True),
        lax.all_gather(w_up[0], "dp", axis=1, tiled=True),
        lax.all_gather(mirror_small[1], "dp", axis=0, tiled=True),
        lax.all_gather(mirror_small[3], "dp", axis=1, tiled=True),
    )
    own_weights = (norm_gain[0], full[0], latent_gain[0], full[1])
    mirror_weights = (mirror_small[0], full[2], mirror_small[2], full[3])
    accum_own = tuple((jnp.zeros(v.shape, jnp.float32) for v in own_weights))
    accum_mirror = tuple((jnp.zeros(v.shape, jnp.float32) for v in mirror_weights))
    state_a = enter_a[0]
    state_b = enter_b[0]
    grad_a = cotan_a[0]
    grad_b = cotan_b[0]
    for tick in range(TICKS):
        out_a = layer(state_a, *own_weights)
        out_b = layer(state_b, *mirror_weights)
        result_a = layer_grads(saved_a[tick, 0], grad_a, own_weights)
        result_b = layer_grads(saved_b[tick, 0], grad_b, mirror_weights)
        back_a = result_a[0]
        back_b = result_b[0]
        accum_own = tuple((p + q.astype(jnp.float32) for p, q in zip(accum_own, result_a[1:])))
        accum_mirror = tuple(
            (p + q.astype(jnp.float32) for p, q in zip(accum_mirror, result_b[1:]))
        )
        if tick < TICKS - 1:
            state_a = from_behind(out_a, "section", 1)
            state_b = from_behind(out_b, "section", -1)
            grad_a = from_behind(back_a, "section", -1)
            grad_b = from_behind(back_b, "section", 1)
    part_own = tuple((v.astype(jnp.bfloat16) for v in accum_own))
    part_mirror = tuple((v.astype(jnp.bfloat16) for v in accum_mirror))
    paired = tuple((jnp.stack([p, q]) for p, q in zip(part_own, part_mirror)))
    sums = (
        lax.psum_scatter(paired[0], "dp", scatter_dimension=1, tiled=True).astype(jnp.float32),
        lax.psum_scatter(paired[1], "dp", scatter_dimension=1, tiled=True).astype(jnp.float32),
        lax.psum_scatter(paired[2], "dp", scatter_dimension=1, tiled=True).astype(jnp.float32),
        lax.psum_scatter(paired[3], "dp", scatter_dimension=2, tiled=True).astype(jnp.float32),
    )
    mine = tuple((v[0] for v in sums))
    theirs = tuple((v[1] for v in sums))
    arrived = theirs
    for bit in range(section_bits):
        arrived = swapped(
            (
                shortened(arrived[0]),
                shortened(arrived[1]),
                shortened(arrived[2]),
                shortened(arrived[3]),
            ),
            "section",
            bit,
        )
    totals = tuple((p + q for p, q in zip(mine, arrived)))
    return (
        out_a[None],
        out_b[None],
        back_a[None],
        back_b[None],
        totals[0][None],
        totals[1][None],
        totals[2][None],
        totals[3][None],
    )


def solution(mesh):
    placed = (
        P("section", "dp", None),
        P("section", "dp", None),
        P("section", "dp", None),
        P("section", "dp", None),
        P(None, "section", "dp", None),
        P(None, "section", "dp", None),
        P("section", None),
        P("section", "dp", None),
        P("section", None),
        P("section", None, "dp"),
    )
    return jax.shard_map(
        body,
        mesh=mesh,
        in_specs=placed,
        out_specs=(
            P("section", "dp", None),
            P("section", "dp", None),
            P("section", "dp", None),
            P("section", "dp", None),
            P("section", "dp"),
            P("section", "dp", None),
            P("section", "dp"),
            P("section", None, "dp"),
        ),
        check_vma=False,
    )
```

profile of v0, /device:TPU:0, one launch (start us, length us, event | category | flops | bytes accessed | tf_op | source)
XLA Modules:
  0.0 882.6 jit_solution(12329885674693998641)
XLA Ops:
  8.7 2.1 collective-permute-start.4
  10.8 5.8 collective-permute-done.4
  18.2 5.2 collective-permute-done.5
  23.4 3.1 collective-permute-start.6
  26.5 4.4 collective-permute-done.6
  33.2 4.8 collective-permute-done.10
  39.4 4.6 collective-permute-done.11
  44.1 4.3 collective-permute-start.12
  48.4 4.0 collective-permute-done.12
  56.7 1.9 fusion.62
  58.6 1.9 fusion.66
  64.3 3.9 collective-permute-start.9
  68.2 2.3 collective-permute-start.3
  70.5 3.0 collective-permute-done.3
  73.6 3.5 multiply_reduce_fusion.11
  77.1 45.5 %all-gather.11.cloned.1.call-done = bf16[1,256,7168]{1,2,0:T(8,128)(2,1)} async-done(((bf16[1,256,448]{1,2,0:T(8,128)(2,1)}), bf16[1,256,7168]{1,2,0:T(8,128)(2,1)}) %all-gather.11.cloned.1.call-update) | async-done | bytes 3670032 | tf_op jit(solution)/shard_map/all_gather | solution.py:60
  122.7 2.9 multiply_reduce_fusion.3
  125.8 3.8 fusion.45
  129.6 2.4 fusion.52
  134.6 4.2 fusion.8
  138.8 78.3 %all-gather.13.cloned.1.call-done = bf16[1,7168,256]{2,1,0:T(8,128)(2,1)} async-done(((bf16[1,448,256]{2,1,0:T(8,128)(2,1)}), bf16[1,7168,256]{2,1,0:T(8,128)(2,1)}) %all-gather.13.cloned.1.call-update) | async-done | bytes 3670032 | tf_op jit(solution)/shard_map/all_gather | solution.py:61
  217.1 3.5 multiply_reduce_fusion.7
  220.6 52.1 %all-gather.15.cloned.1.call-done = bf16[1,256,7168]{1,2,0:T(8,128)(2,1)} async-done(((bf16[1,256,448]{1,2,0:T(8,128)(2,1)}), bf16[1,256,7168]{1,2,0:T(8,128)(2,1)}) %all-gather.15.cloned.1.call-update) | async-done | bytes 3670032 | tf_op jit(solution)/shard_map/all_gather | solution.py:62
  272.7 2.9 multiply_reduce_fusion.1
  275.9 3.8 fusion.41
  280.9 2.7 collective-permute-start.15
  286.9 2.8 fusion.17
  289.7 33.4 %collective-permute-done.15 = bf16[128,7168]{1,0:T(8,128)(2,1)S(1)} collective-permute-done((bf16[128,7168]{1,0:T(8,128)(2,1)S(1)}, bf16[128,7168]{1,0:T(8,128)(2,1)S(1)}, u32[]{:S(2)}, u32[]{:S(2)}) %collective-permute-start.15) | collective-permute-done | bytes 1835040 | tf_op jit(solution)/shard_map/ppermute | solution.py:16
  325.5 3.7 pad_maximum_fusion.1
  329.2 18.5 %copy.21 = bf16[2,256,7168]{1,0,2:T(2,128)(2,1)} copy(bf16[2,256,7168]{2,1,0:T(8,128)(2,1)} %pad_maximum_fusion.1) | data formatting | bytes 14680064 | tf_op jit(solution)/shard_map/stack | solution.py:90
  348.0 3.5 multiply_reduce_fusion.2
  351.6 5.4 fusion.43
  358.4 3.3 fusion.19
  364.5 3.4 fusion.39
  369.8 2.9 fusion.7
  372.7 3.2 fusion.18
  376.0 6.8 pad_maximum_fusion
  383.1 2.0 fusion.56
  385.0 3.5 multiply_reduce_fusion.15
  389.3 2.5 fusion.20
  391.9 5.8 collective-permute-start
  398.9 2.0 fusion.59
  400.9 3.6 multiply_reduce_fusion.13
  405.2 2.5 fusion.22
  409.0 103.3 %collective-permute-done = bf16[128,7168]{1,0:T(8,128)(2,1)} collective-permute-done((bf16[128,7168]{1,0:T(8,128)(2,1)}, bf16[128,7168]{1,0:T(8,128)(2,1)}, u32[]{:S(2)}, u32[]{:S(2)}) %collective-permute-start) | collective-permute-done | bytes 1835040 | tf_op jit(solution)/shard_map/ppermute | solution.py:16
  512.4 1.9 fusion.46
  514.3 2.4 multiply_reduce_fusion.14
  516.9 4.2 fusion.29
  521.1 3.9 fusion.105
  525.8 2.0 fusion.49
  527.9 3.4 multiply_reduce_fusion.12
  531.3 5.0 fusion.104
  536.3 68.5 %all-reduce.3.cloned.1.call-done = bf16[2,256,7168]{1,0,2:T(2,128)(2,1)} async-done(((bf16[2,256,7168]{1,0,2:T(2,128)(2,1)}), bf16[2,256,7168]{1,0,2:T(2,128)(2,1)}) %all-reduce.3.cloned.1.call-update) | async-done | bytes 7340048
  604.9 1.9 constant_dynamic-slice_fusion
  606.9 73.6 %reduce-scatter.10.cloned.1.call-done = bf16[448,2]{1,0:T(8,128)(2,1)} async-done(((bf16[7168,2]{1,0:T(8,128)(2,1)}), bf16[448,2]{1,0:T(8,128)(2,1)}) %reduce-scatter.10.cloned.1.call-update) | async-done | bytes 1808
  684.0 94.5 %reduce-scatter.8.cloned.1.call-done = bf16[2,448,256]{2,1,0:T(8,128)(2,1)} async-done(((bf16[2,7168,256]{2,1,0:T(8,128)(2,1)}), bf16[2,448,256]{2,1,0:T(8,128)(2,1)}) %reduce-scatter.8.cloned.1.call-update) | async-done | bytes 458768 | tf_op jit(solution)/shard_map/reduce_scatter | solution.py:93
  780.4 5.2 fusion.28
  787.1 55.9 %reduce-scatter.12.cloned.1.call-done = bf16[16,2]{1,0:T(8,128)(2,1)} async-done(((bf16[256,2]{1,0:T(8,128)(2,1)}), bf16[16,2]{1,0:T(8,128)(2,1)}) %reduce-scatter.12.cloned.1.call-update) | async-done | bytes 80
  844.8 2.7 collective-permute-done.22
  849.0 2.1 collective-permute-done.23
  851.1 3.0 collective-permute-start.24
  854.7 3.0 collective-permute-start.27
  859.8 7.4 collective-permute-done.20
  869.4 5.3 collective-permute-done.21
  (169 shorter events, 51.9 us)
Async XLA Ops:
  7.2 66.4 %copy-start.17 = (f32[1,7168]{1,0:T(1,128)S(1)}, f32[1,7168]{1,0:T(1,128)}, u32[]{:S(2)}) copy-start(f32[1,7168]{1,0:T(1,128)} %param.16) | copy-start | bytes 86020
  7.2 66.4 %all-gather.9.cloned.1.call-start = ((), (), s32[]{:S(2)}) async-start(), calls=%async_computation.4 | async-start | bytes 3899392 | tf_op jit(solution)/shard_map/all_gather | solution.py:59
  7.9 114.7 %all-gather.11.cloned.1.call-start = ((), (), s32[]{:S(2)}) async-start(), calls=%async_computation.5 | async-start | bytes 3899392 | tf_op jit(solution)/shard_map/all_gather | solution.py:60
  8.7 208.4 %all-gather.13.cloned.1.call-start = ((), (), s32[]{:S(2)}) async-start(), calls=%async_computation.6 | async-start | bytes 3899392 | tf_op jit(solution)/shard_map/all_gather | solution.py:61
  8.7 7.9 collective-permute-start.4
  16.6 6.8 collective-permute-start.5
  23.4 7.5 collective-permute-start.6
  30.9 0.7 copy-start.19
  31.6 241.1 %all-gather.15.cloned.1.call-start = ((), (), s32[]{:S(2)}) async-start(), calls=%async_computation.7 | async-start | bytes 3899392 | tf_op jit(solution)/shard_map/all_gather | solution.py:62
  31.7 6.3 collective-permute-start.10
  38.0 6.1 collective-permute-start.11
  44.1 8.3 collective-permute-start.12
  53.1 551.8 %all-reduce.3.cloned.1.call-start = ((), (), s32[]{:S(2)}) async-start(), calls=%async_computation.10 | async-start | bytes 14680064
  53.9 8.5 collective-permute-start.1
  56.5 4.1 collective-permute-start.7
  60.6 3.6 collective-permute-start.8
  62.4 5.8 collective-permute-start.2
  64.3 6.2 collective-permute-start.9
  68.2 5.4 collective-permute-start.3
  73.6 49.0 %copy-start.10 = (bf16[1,128,7168]{2,1,0:T(8,128)(2,1)S(1)}, bf16[1,128,7168]{2,1,0:T(8,128)(2,1)}, u32[]{:S(2)}) copy-start(bf16[1,128,7168]{2,1,0:T(8,128)(2,1)} %param.12) | copy-start | bytes 5505028
  73.6 49.0 %copy-start.21 = (f32[1,256]{1,0:T(1,128)S(1)}, f32[1,256]{1,0:T(1,128)}, u32[]{:S(2)}) copy-start(f32[1,256]{1,0:T(1,128)} %param.18) | copy-start | bytes 3076
  122.6 3.1 copy-start.4
  129.6 4.3 copy-start.22
  132.0 153.6 %collective-permute-start.14 = (bf16[128,7168]{1,0:T(8,128)(2,1)}, bf16[128,7168]{1,0:T(8,128)(2,1)}, u32[]{:S(2)}, u32[]{:S(2)}) collective-permute-start(bf16[128,7168]{1,0:T(8,128)(2,1)} %fusion.52), channel_id=1, source_target_pairs={{16,0},{32,16},{48,32},{64,48},{80,64},{96,80},{112,96},{17,1},{33... | collective-permute-start | bytes 5505032 | tf_op jit(solution)/shard_map/ppermute | solution.py:16
  217.1 55.7 %copy-start.11 = (bf16[1,128,7168]{2,1,0:T(8,128)(2,1)S(1)}, bf16[1,128,7168]{2,1,0:T(8,128)(2,1)}, u32[]{:S(2)}) copy-start(bf16[1,128,7168]{2,1,0:T(8,128)(2,1)} %param.13) | copy-start | bytes 5505028
  272.7 3.1 copy-start.7
  279.6 3.9 copy-start.24
  280.9 42.2 %collective-permute-start.15 = (bf16[128,7168]{1,0:T(8,128)(2,1)S(1)}, bf16[128,7168]{1,0:T(8,128)(2,1)S(1)}, u32[]{:S(2)}, u32[]{:S(2)}) collective-permute-start(bf16[128,7168]{1,0:T(8,128)(2,1)S(1)} %fusion.54), channel_id=1, source_target_pairs={{0,16},{16,32},{32,48},{48,64},{64,80},{80,96},{96,112},{1,17},{17... | collective-permute-start | bytes 5505032 | tf_op jit(solution)/shard_map/ppermute | solution.py:16
  283.6 2.2 slice-start
  284.4 2.6 slice-start.1
  323.1 1.2 copy-start.12
  347.7 332.8 %reduce-scatter.10.cloned.1.call-start = ((), (), s32[]{:S(2)}) async-start(), calls=%async_computation.8 | async-start | bytes 1949696
  348.0 3.7 copy-start.5
  358.3 3.4 copy-start
  358.4 3.4 copy-start.13
  358.4 5.0 copy-start.25
  361.7 2.8 copy-start.8
  369.8 2.9 copy-start.9
  375.9 402.6 %reduce-scatter.8.cloned.1.call-start = ((), (), s32[]{:S(2)}) async-start(), calls=%async_computation.3 | async-start | bytes 7798784 | tf_op jit(solution)/shard_map/reduce_scatter | solution.py:93
  382.8 460.2 %reduce-scatter.12.cloned.1.call-start = ((), (), s32[]{:S(2)}) async-start(), calls=%async_computation.9 | async-start | bytes 69632
  385.0 3.7 copy-start.2
  385.0 4.3 copy-start.14
  389.3 8.3 copy-start.26
  391.9 120.5 %collective-permute-start = (bf16[128,7168]{1,0:T(8,128)(2,1)}, bf16[128,7168]{1,0:T(8,128)(2,1)}, u32[]{:S(2)}, u32[]{:S(2)}) collective-permute-start(bf16[128,7168]{1,0:T(8,128)(2,1)} %fusion.20), channel_id=1, source_target_pairs={{0,16},{16,32},{32,48},{48,64},{64,80},{80,96},{96,112},{1,17},{17... | collective-permute-start | bytes 5505032 | tf_op jit(solution)/shard_map/ppermute | solution.py:16
  400.8 3.8 copy-start.1
  400.9 4.3 copy-start.15
  405.2 109.2 %copy-start.23 = (bf16[1,7168,256]{2,1,0:T(8,128)(2,1)S(1)}, bf16[1,7168,256]{2,1,0:T(8,128)(2,1)}, u32[]{:S(2)}) copy-start(bf16[1,7168,256]{2,1,0:T(8,128)(2,1)} %all-gather.9.cloned.1.call-done) | copy-start | bytes 11010052
  407.7 118.1 %collective-permute-start.13 = (bf16[128,7168]{1,0:T(8,128)(2,1)}, bf16[128,7168]{1,0:T(8,128)(2,1)}, u32[]{:S(2)}, u32[]{:S(2)}) collective-permute-start(bf16[128,7168]{1,0:T(8,128)(2,1)} %fusion.22), channel_id=1, source_target_pairs={{16,0},{32,16},{48,32},{64,48},{80,64},{96,80},{112,96},{17,1},{33... | collective-permute-start | bytes 5505032 | tf_op jit(solution)/shard_map/ppermute | solution.py:16
  514.3 2.6 copy-start.3
  516.9 4.2 copy-start.6
  516.9 4.2 copy-start.16
  606.8 75.7 %collective-permute-start.25 = (bf16[256,448]{0,1:T(8,128)(2,1)S(1)}, bf16[256,448]{0,1:T(8,128)(2,1)S(1)}, u32[]{:S(2)}, u32[]{:S(2)}) collective-permute-start(bf16[256,448]{0,1:T(8,128)(2,1)S(1)} %bitcast.261), channel_id=1, source_target_pairs={{0,16},{16,0},{32,48},{48,32},{64,80},{80,64},{96,112},{112,96},{1... | collective-permute-start | bytes 688136 | tf_op jit(solution)/shard_map/ppermute | solution.py:10
  681.7 104.0 %collective-permute-start.16 = (bf16[448]{0:T(512)(128)(2,1)S(1)}, bf16[448]{0:T(512)(128)(2,1)S(1)}, u32[]{:S(2)}, u32[]{:S(2)}) collective-permute-start(bf16[448]{0:T(512)(128)(2,1)S(1)} %get-tuple-element.36), channel_id=1, source_target_pairs={{0,16},{16,0},{32,48},{48,32},{64,80},{80,64},{96,112},{112,96},{1... | collective-permute-start | bytes 2696 | tf_op jit(solution)/shard_map/ppermute | solution.py:10
  682.5 172.1 %collective-permute-start.26 = (bf16[256,448]{0,1:T(8,128)(2,1)S(1)}, bf16[256,448]{0,1:T(8,128)(2,1)S(1)}, u32[]{:S(2)}, u32[]{:S(2)}) collective-permute-start(bf16[256,448]{0,1:T(8,128)(2,1)S(1)} %collective-permute-done.25), channel_id=1, source_target_pairs={{0,32},{16,48},{32,0},{48,16},{64,96},{80,112},{96,64},{112,80},{1... | collective-permute-start | bytes 688136 | tf_op jit(solution)/shard_map/ppermute | solution.py:10
  779.5 78.2 %collective-permute-start.19 = (bf16[448,256]{1,0:T(8,128)(2,1)S(1)}, bf16[448,256]{1,0:T(8,128)(2,1)S(1)}, u32[]{:S(2)}, u32[]{:S(2)}) collective-permute-start(bf16[448,256]{1,0:T(8,128)(2,1)S(1)} %slice_bitcast_fusion), channel_id=1, source_target_pairs={{0,16},{16,0},{32,48},{48,32},{64,80},{80,64},{96,112},{112,96},{1... | collective-permute-start | bytes 688136 | tf_op jit(solution)/shard_map/ppermute | solution.py:10
  780.4 94.2 %copy-start.18 = (bf16[2,448,256]{2,1,0:T(8,128)(2,1)S(1)}, bf16[2,448,256]{2,1,0:T(8,128)(2,1)}, u32[]{:S(2)}) copy-start(bf16[2,448,256]{2,1,0:T(8,128)(2,1)} %reduce-scatter.8.cloned.1.call-done) | copy-start | bytes 1376260
  785.6 68.5 %collective-permute-start.17 = (bf16[448]{0:T(512)(128)(2,1)S(1)}, bf16[448]{0:T(512)(128)(2,1)S(1)}, u32[]{:S(2)}, u32[]{:S(2)}) collective-permute-start(bf16[448]{0:T(512)(128)(2,1)S(1)} %collective-permute-done.16), channel_id=1, source_target_pairs={{0,32},{16,48},{32,0},{48,16},{64,96},{80,112},{96,64},{112,80},{1... | collective-permute-start | bytes 2696 | tf_op jit(solution)/shard_map/ppermute | solution.py:10
  844.0 3.5 collective-permute-start.22
  847.6 3.5 collective-permute-start.23
  851.1 7.1 collective-permute-start.24
  854.1 5.1 collective-permute-start.18
  854.7 13.9 %collective-permute-start.27 = (bf16[256,448]{0,1:T(8,128)(2,1)S(1)}, bf16[256,448]{0,1:T(8,128)(2,1)S(1)}, u32[]{:S(2)}, u32[]{:S(2)}) collective-permute-start(bf16[256,448]{0,1:T(8,128)(2,1)S(1)} %collective-permute-done.26), channel_id=1, source_target_pairs={{0,64},{16,80},{32,96},{48,112},{64,0},{80,16},{96,32},{112,48},{1... | collective-permute-start | bytes 688136 | tf_op jit(solution)/shard_map/ppermute | solution.py:10
  857.6 9.5 %collective-permute-start.20 = (bf16[448,256]{1,0:T(8,128)(2,1)S(1)}, bf16[448,256]{1,0:T(8,128)(2,1)S(1)}, u32[]{:S(2)}, u32[]{:S(2)}) collective-permute-start(bf16[448,256]{1,0:T(8,128)(2,1)S(1)} %collective-permute-done.19), channel_id=1, source_target_pairs={{0,32},{16,48},{32,0},{48,16},{64,96},{80,112},{96,64},{112,80},{1... | collective-permute-start | bytes 688136 | tf_op jit(solution)/shard_map/ppermute | solution.py:10
  867.2 7.5 collective-permute-start.21
  (1 other events, 0.7 us)
Sparse Core Ops, SparseCore 0:
  10.4 56.9 all-gather.8
  69.8 52.7 all-gather.10
  125.6 91.4 all-gather.12
  219.9 52.7 all-gather.14
  347.9 256.9 all-reduce.2
  608.6 71.8 reduce-scatter.9
  685.3 93.1 reduce-scatter.7
  782.6 60.3 reduce-scatter.11
where the time goes:
time: 890 us; the launch traced here: 883 us
  waiting for transfers between devices  658 us (74%)
  matrix products  82.5 us (9%)
  starting transfers between devices  52.4 us (6%)
  other arithmetic  40.5 us (5%)
  local copies, waits for them, and re-layouts  33.8 us (4%)
  between operations  15.5 us (2%)
    unnamed x11, waiting for transfers between devices  199 us
    ppermute x4, waiting for transfers between devices, from_behind(): return lax.ppermute(block, axis, route)  137 us
    reduce_scatter x1, waiting for transfers between devices, body(): lax.psum_scatter(paired[1], 'dp', scatter_dimension=1, tiled=True)  94.5 us
    all_gather x1, waiting for transfers between devices, body(): lax.all_gather(mirror_small[1], 'dp', axis=0, tiled=True)  78.3 us
    all_gather x1, waiting for transfers between devices, body(): lax.all_gather(mirror_small[3], 'dp', axis=1, tiled=True)  52.1 us
    ppermute x24, waiting for transfers between devices, swapped(): lax.ppermute(value, axis, [(i, i ^ 1 << distance) for i in range(lax.axis...  51.3 us
    dot_general x16, matrix products, layer(): latent = jnp.dot(normed, w_down, preferred_element_type=jnp.float32)  48.5 us
    all_gather x1, waiting for transfers between devices, body(): lax.all_gather(w_up[0], 'dp', axis=1, tiled=True)  45.5 us
  transfers between devices with their start and end apart: 36, of which 22 were waited for; matrix products, arithmetic and copies ran while one was open for 14% of the time, Pallas kernels for 0%

commit v1 on v0

--- a/solution.py
+++ b/solution.py
@@ -59,7 +59,9 @@
         lax.all_gather(w_down[0], "dp", axis=0, tiled=True),
         lax.all_gather(w_up[0], "dp", axis=1, tiled=True),
         lax.all_gather(mirror_small[1], "dp", axis=0, tiled=True),
-        lax.all_gather(mirror_small[3], "dp", axis=1, tiled=True),
+        jnp.concatenate(
+            lax.all_to_all(jnp.stack([mirror_small[3]] * lax.axis_size("dp")), "dp", 0, 0), axis=1
+        ),
     )
     own_weights = (norm_gain[0], full[0], latent_gain[0], full[1])
     mirror_weights = (mirror_small[0], full[2], mirror_small[2], full[3])

time: 890 us -> 857 us (0.963)
  waiting for transfers between devices: 658 us -> 616 us
    all_gather x1 -> x0, waiting for transfers between devices: 52.1 us -> none  [body(): lax.all_gather(mirror_small[3], 'dp', axis=1, tiled=True)]
    all_gather x1, waiting for transfers between devices: 45.5 us -> 69 us  [body(): lax.all_gather(w_up[0], 'dp', axis=1, tiled=True)]
    ppermute x24, waiting for transfers between devices: 51.3 us -> 36 us  [swapped(): lax.ppermute(value, axis, [(i, i ^ 1 << distance) for i in range(lax.axis...]
    unnamed x11 -> x10, waiting for transfers between devices: 199 us -> 200 us
  transfers between devices with their start and end apart: 36 -> 36, of which waited for: 22 -> 20; matrix products, arithmetic and copies ran while one was open for 14% -> 15% of each run, Pallas kernels for 0% -> 0%
where the time goes in v1:
time: 857 us; the launch traced here: 850 us
  waiting for transfers between devices  616 us (72%)
  matrix products  86.7 us (10%)
  starting transfers between devices  58 us (7%)
  other arithmetic  40.5 us (5%)
  local copies, waits for them, and re-layouts  32.9 us (4%)
  between operations  15.5 us (2%)
    unnamed x10, waiting for transfers between devices  200 us
    ppermute x4, waiting for transfers between devices, from_behind(): return lax.ppermute(block, axis, route)  135 us
    reduce_scatter x1, waiting for transfers between devices, body(): lax.psum_scatter(paired[1], 'dp', scatter_dimension=1, tiled=True)  94.4 us
    all_gather x1, waiting for transfers between devices, body(): lax.all_gather(mirror_small[1], 'dp', axis=0, tiled=True)  80.2 us
    all_gather x1, waiting for transfers between devices, body(): lax.all_gather(w_up[0], 'dp', axis=1, tiled=True)  69 us
    dot_general x16, matrix products, layer(): latent = jnp.dot(normed, w_down, preferred_element_type=jnp.float32)  48.5 us
    dot_general x12, matrix products, layer(): jnp.dot(scaled, w_up, preferred_element_type=jnp.float32)  38.3 us
    ppermute x24, starting transfers between devices, swapped(): lax.ppermute(value, axis, [(i, i ^ 1 << distance) for i in range(lax.axis...  37.8 us
  transfers between devices with their start and end apart: 36, of which 20 were waited for; matrix products, arithmetic and copies ran while one was open for 15% of the time, Pallas kernels for 0%

profile of v1, /device:TPU:0, one launch (start us, length us, event | category | flops | bytes accessed | tf_op | source)
XLA Modules:
  0.0 849.6 jit_solution(6872794126661629561)
XLA Ops:
  8.7 2.1 collective-permute-start.4
  10.8 5.8 collective-permute-done.4
  18.2 5.2 collective-permute-done.5
  23.4 3.1 collective-permute-start.6
  26.5 4.4 collective-permute-done.6
  36.7 1.9 fusion.62
  38.6 1.7 collective-permute-start.11
  40.3 1.9 fusion.66
  45.3 4.3 collective-permute-start.12
  49.6 3.4 collective-permute-start.3
  55.1 2.3 stack.31
  57.3 8.1 all-to-all-start
  67.1 3.5 multiply_reduce_fusion.11
  70.6 69.0 %all-gather.9.cloned.1.call-done = bf16[1,256,7168]{1,2,0:T(8,128)(2,1)} async-done(((bf16[1,256,448]{1,2,0:T(8,128)(2,1)}), bf16[1,256,7168]{1,2,0:T(8,128)(2,1)}) %all-gather.9.cloned.1.call-update) | async-done | bytes 3670032 | tf_op jit(solution)/shard_map/all_gather | solution.py:60
  139.7 2.9 multiply_reduce_fusion.3
  142.8 3.7 fusion.45
  146.6 2.4 fusion.52
  149.0 1.8 collective-permute-start.14
  151.6 4.2 fusion.8
  155.8 80.2 %all-gather.11.cloned.1.call-done = bf16[1,7168,256]{2,1,0:T(8,128)(2,1)} async-done(((bf16[1,448,256]{2,1,0:T(8,128)(2,1)}), bf16[1,7168,256]{2,1,0:T(8,128)(2,1)}) %all-gather.11.cloned.1.call-update) | async-done | bytes 3670032 | tf_op jit(solution)/shard_map/all_gather | solution.py:61
  236.0 3.5 multiply_reduce_fusion.7
  239.6 2.9 multiply_reduce_fusion.1
  242.7 3.8 fusion.41
  247.7 2.7 collective-permute-start.15
  253.8 2.8 fusion.17
  256.5 33.4 %collective-permute-done.15 = bf16[128,7168]{1,0:T(8,128)(2,1)S(1)} collective-permute-done((bf16[128,7168]{1,0:T(8,128)(2,1)S(1)}, bf16[128,7168]{1,0:T(8,128)(2,1)S(1)}, u32[]{:S(2)}, u32[]{:S(2)}) %collective-permute-start.15) | collective-permute-done | bytes 1835040 | tf_op jit(solution)/shard_map/ppermute | solution.py:16
  292.4 3.7 pad_maximum_fusion.1
  296.0 18.5 %copy.23 = bf16[2,256,7168]{1,0,2:T(2,128)(2,1)} copy(bf16[2,256,7168]{2,1,0:T(8,128)(2,1)} %pad_maximum_fusion.1) | data formatting | bytes 14680064 | tf_op jit(solution)/shard_map/stack | solution.py:92
  314.8 3.5 multiply_reduce_fusion.2
  318.5 5.4 fusion.43
  325.2 3.3 fusion.19
  328.5 2.9 multiply_reduce_fusion
  331.7 3.4 fusion.39
  335.2 1.7 copy.26
  336.9 2.9 fusion.7
  339.8 3.2 fusion.18
  343.1 6.8 pad_maximum_fusion
  350.2 2.0 fusion.56
  352.2 3.5 multiply_reduce_fusion.15
  356.5 2.5 fusion.20
  359.0 5.8 collective-permute-start
  366.0 2.0 fusion.59
  368.0 3.5 multiply_reduce_fusion.13
  371.6 4.7 fusion.22
  377.6 101.6 %collective-permute-done = bf16[128,7168]{1,0:T(8,128)(2,1)} collective-permute-done((bf16[128,7168]{1,0:T(8,128)(2,1)}, bf16[128,7168]{1,0:T(8,128)(2,1)}, u32[]{:S(2)}, u32[]{:S(2)}) %collective-permute-start) | collective-permute-done | bytes 1835040 | tf_op jit(solution)/shard_map/ppermute | solution.py:16
  479.2 1.9 fusion.46
  481.2 2.4 multiply_reduce_fusion.14
  483.8 4.2 fusion.29
  488.0 3.9 fusion.99
  492.7 2.0 fusion.49
  494.7 3.4 multiply_reduce_fusion.12
  498.2 5.0 fusion.98
  503.2 68.8 %all-reduce.3.cloned.1.call-done = bf16[2,256,7168]{1,0,2:T(2,128)(2,1)} async-done(((bf16[2,256,7168]{1,0,2:T(2,128)(2,1)}), bf16[2,256,7168]{1,0,2:T(2,128)(2,1)}) %all-reduce.3.cloned.1.call-update) | async-done | bytes 7340048
  572.0 1.9 constant_dynamic-slice_fusion
  574.0 73.5 %reduce-scatter.10.cloned.1.call-done = bf16[448,2]{1,0:T(8,128)(2,1)} async-done(((bf16[7168,2]{1,0:T(8,128)(2,1)}), bf16[448,2]{1,0:T(8,128)(2,1)}) %reduce-scatter.10.cloned.1.call-update) | async-done | bytes 1808
  651.1 94.4 %reduce-scatter.8.cloned.1.call-done = bf16[2,448,256]{2,1,0:T(8,128)(2,1)} async-done(((bf16[2,7168,256]{2,1,0:T(8,128)(2,1)}), bf16[2,448,256]{2,1,0:T(8,128)(2,1)}) %reduce-scatter.8.cloned.1.call-update) | async-done | bytes 458768 | tf_op jit(solution)/shard_map/reduce_scatter | solution.py:95
  747.4 5.2 fusion.28
  754.1 55.9 %reduce-scatter.12.cloned.1.call-done = bf16[16,2]{1,0:T(8,128)(2,1)} async-done(((bf16[256,2]{1,0:T(8,128)(2,1)}), bf16[16,2]{1,0:T(8,128)(2,1)}) %reduce-scatter.12.cloned.1.call-update) | async-done | bytes 80
  811.9 2.7 collective-permute-done.22
  816.0 2.1 collective-permute-done.23
  818.1 3.0 collective-permute-start.24
  821.6 3.0 collective-permute-start.27
  826.8 7.4 collective-permute-done.20
  836.4 5.3 collective-permute-done.21
  (163 shorter events, 46.0 us)
Async XLA Ops:
  7.2 59.9 %all-gather.7.cloned.1.call-start = ((), (), s32[]{:S(2)}) async-start(), calls=%async_computation.5 | async-start | bytes 3899392 | tf_op jit(solution)/shard_map/all_gather | solution.py:59
  7.9 131.7 %all-gather.9.cloned.1.call-start = ((), (), s32[]{:S(2)}) async-start(), calls=%async_computation.6 | async-start | bytes 3899392 | tf_op jit(solution)/shard_map/all_gather | solution.py:60
  8.7 227.4 %all-gather.11.cloned.1.call-start = ((), (), s32[]{:S(2)}) async-start(), calls=%async_computation.7 | async-start | bytes 3899392 | tf_op jit(solution)/shard_map/all_gather | solution.py:61
  8.7 7.9 collective-permute-start.4
  16.6 6.8 collective-permute-start.5
  23.4 7.5 collective-permute-start.6
  30.9 0.7 copy-start.17
  31.6 7.0 collective-permute-start.10
  33.9 8.9 %collective-permute-start.1 = (bf16[1,7168]{1,0:T(2,128)(2,1)S(1)}, bf16[1,7168]{1,0:T(2,128)(2,1)S(1)}, u32[]{:S(2)}, u32[]{:S(2)}) collective-permute-start(bf16[1,7168]{1,0:T(2,128)(2,1)S(1)} %convert_element_type.345), channel_id=1, source_target_pairs={{0,16},{16,0},{32,48},{48,32},{64,80},{80,64},{96,112},{112,96},{1... | collective-permute-start | bytes 43016 | tf_op jit(solution)/shard_map/ppermute | solution.py:10
  35.2 7.0 collective-permute-start.7
  38.6 6.6 collective-permute-start.11
  42.2 7.3 collective-permute-start.8
  42.8 6.9 collective-permute-start.2
  45.3 9.8 %collective-permute-start.12 = (bf16[1,256,448]{1,2,0:T(8,128)(2,1)S(1)}, bf16[1,256,448]{1,2,0:T(8,128)(2,1)S(1)}, u32[]{:S(2)}, u32[]{:S(2)}) collective-permute-start(bf16[1,256,448]{1,2,0:T(8,128)(2,1)S(1)} %collective-permute-done.11), channel_id=1, source_target_pairs={{0,64},{16,80},{32,96},{48,112},{64,0},{80,16},{96,32},{112,48},{1... | collective-permute-start | bytes 688136 | tf_op jit(solution)/shard_map/ppermute | solution.py:10
  49.6 5.1 collective-permute-start.9
  49.6 5.4 collective-permute-start.3
  57.3 9.8 %copy-start.15 = (f32[1,7168]{1,0:T(1,128)S(1)}, f32[1,7168]{1,0:T(1,128)}, u32[]{:S(2)}) copy-start(f32[1,7168]{1,0:T(1,128)} %param.16) | copy-start | bytes 86020
  57.3 182.2 %all-to-all-start = ((bf16[16,256,448]{1,2,0:T(8,128)(2,1)}), bf16[16,256,448]{1,2,0:T(8,128)(2,1)}, u32[]{:S(2)}, u32[]{:S(2)}) async-start(bf16[16,256,448]{1,2,0:T(8,128)(2,1)} %stack.31), calls=%async_computation | async-start | bytes 7340032 | tf_op jit(solution)/shard_map/all_to_all | solution.py:63
  65.4 506.6 %all-reduce.3.cloned.1.call-start = ((), (), s32[]{:S(2)}) async-start(), calls=%async_computation.10 | async-start | bytes 14680064
  67.1 72.6 %copy-start.8 = (bf16[1,128,7168]{2,1,0:T(8,128)(2,1)S(1)}, bf16[1,128,7168]{2,1,0:T(8,128)(2,1)}, u32[]{:S(2)}) copy-start(bf16[1,128,7168]{2,1,0:T(8,128)(2,1)} %param.12) | copy-start | bytes 5505028
  67.1 72.6 %copy-start.18 = (f32[1,256]{1,0:T(1,128)S(1)}, f32[1,256]{1,0:T(1,128)}, u32[]{:S(2)}) copy-start(f32[1,256]{1,0:T(1,128)} %param.18) | copy-start | bytes 3076
  139.7 3.1 copy-start.2
  146.6 4.3 copy-start.19
  149.0 103.4 %collective-permute-start.14 = (bf16[128,7168]{1,0:T(8,128)(2,1)}, bf16[128,7168]{1,0:T(8,128)(2,1)}, u32[]{:S(2)}, u32[]{:S(2)}) collective-permute-start(bf16[128,7168]{1,0:T(8,128)(2,1)} %fusion.52), channel_id=1, source_target_pairs={{16,0},{32,16},{48,32},{64,48},{80,64},{96,80},{112,96},{17,1},{33... | collective-permute-start | bytes 5505032 | tf_op jit(solution)/shard_map/ppermute | solution.py:16
  236.0 3.5 copy-start.9
  239.5 3.1 copy-start.5
  246.5 3.9 copy-start.21
  247.7 42.2 %collective-permute-start.15 = (bf16[128,7168]{1,0:T(8,128)(2,1)S(1)}, bf16[128,7168]{1,0:T(8,128)(2,1)S(1)}, u32[]{:S(2)}, u32[]{:S(2)}) collective-permute-start(bf16[128,7168]{1,0:T(8,128)(2,1)S(1)} %fusion.54), channel_id=1, source_target_pairs={{0,16},{16,32},{32,48},{48,64},{64,80},{80,96},{96,112},{1,17},{17... | collective-permute-start | bytes 5505032 | tf_op jit(solution)/shard_map/ppermute | solution.py:16
  250.4 2.2 slice-start
  251.2 2.6 slice-start.1
  289.9 1.2 copy-start.10
  314.6 333.0 %reduce-scatter.10.cloned.1.call-start = ((), (), s32[]{:S(2)}) async-start(), calls=%async_computation.8 | async-start | bytes 1949696
  314.8 3.7 copy-start.3
  325.2 3.4 copy-start.11
  325.2 6.3 copy-start.22
  328.5 3.1 copy-start.6
  336.9 2.9 copy-start.7
  343.1 402.4 %reduce-scatter.8.cloned.1.call-start = ((), (), s32[]{:S(2)}) async-start(), calls=%async_computation.4 | async-start | bytes 7798784 | tf_op jit(solution)/shard_map/reduce_scatter | solution.py:95
  349.9 460.1 %reduce-scatter.12.cloned.1.call-start = ((), (), s32[]{:S(2)}) async-start(), calls=%async_computation.9 | async-start | bytes 69632
  352.2 3.7 copy-start
  352.2 4.3 copy-start.12
  356.5 8.3 copy-start.23
  359.0 120.2 %collective-permute-start = (bf16[128,7168]{1,0:T(8,128)(2,1)}, bf16[128,7168]{1,0:T(8,128)(2,1)}, u32[]{:S(2)}, u32[]{:S(2)}) collective-permute-start(bf16[128,7168]{1,0:T(8,128)(2,1)} %fusion.20), channel_id=1, source_target_pairs={{0,16},{16,32},{32,48},{48,64},{64,80},{80,96},{96,112},{1,17},{17... | collective-permute-start | bytes 5505032 | tf_op jit(solution)/shard_map/ppermute | solution.py:16
  368.0 3.6 copy-start.13
  371.6 109.6 %copy-start.20 = (bf16[1,7168,256]{2,1,0:T(8,128)(2,1)S(1)}, bf16[1,7168,256]{2,1,0:T(8,128)(2,1)}, u32[]{:S(2)}) copy-start(bf16[1,7168,256]{2,1,0:T(8,128)(2,1)} %all-gather.7.cloned.1.call-done) | copy-start | bytes 11010052
  376.3 116.4 %collective-permute-start.13 = (bf16[128,7168]{1,0:T(8,128)(2,1)}, bf16[128,7168]{1,0:T(8,128)(2,1)}, u32[]{:S(2)}, u32[]{:S(2)}) collective-permute-start(bf16[128,7168]{1,0:T(8,128)(2,1)} %fusion.22), channel_id=1, source_target_pairs={{16,0},{32,16},{48,32},{64,48},{80,64},{96,80},{112,96},{17,1},{33... | collective-permute-start | bytes 5505032 | tf_op jit(solution)/shard_map/ppermute | solution.py:16
  481.2 2.6 copy-start.1
  483.8 4.2 copy-start.4
  483.8 4.2 copy-start.14
  573.9 75.7 %collective-permute-start.25 = (bf16[256,448]{0,1:T(8,128)(2,1)S(1)}, bf16[256,448]{0,1:T(8,128)(2,1)S(1)}, u32[]{:S(2)}, u32[]{:S(2)}) collective-permute-start(bf16[256,448]{0,1:T(8,128)(2,1)S(1)} %bitcast.248), channel_id=1, source_target_pairs={{0,16},{16,0},{32,48},{48,32},{64,80},{80,64},{96,112},{112,96},{1... | collective-permute-start | bytes 688136 | tf_op jit(solution)/shard_map/ppermute | solution.py:10
  648.7 103.9 %collective-permute-start.16 = (bf16[448]{0:T(512)(128)(2,1)S(1)}, bf16[448]{0:T(512)(128)(2,1)S(1)}, u32[]{:S(2)}, u32[]{:S(2)}) collective-permute-start(bf16[448]{0:T(512)(128)(2,1)S(1)} %get-tuple-element.44), channel_id=1, source_target_pairs={{0,16},{16,0},{32,48},{48,32},{64,80},{80,64},{96,112},{112,96},{1... | collective-permute-start | bytes 2696 | tf_op jit(solution)/shard_map/ppermute | solution.py:10
  649.6 172.0 %collective-permute-start.26 = (bf16[256,448]{0,1:T(8,128)(2,1)S(1)}, bf16[256,448]{0,1:T(8,128)(2,1)S(1)}, u32[]{:S(2)}, u32[]{:S(2)}) collective-permute-start(bf16[256,448]{0,1:T(8,128)(2,1)S(1)} %collective-permute-done.25), channel_id=1, source_target_pairs={{0,32},{16,48},{32,0},{48,16},{64,96},{80,112},{96,64},{112,80},{1... | collective-permute-start | bytes 688136 | tf_op jit(solution)/shard_map/ppermute | solution.py:10
  746.5 78.2 %collective-permute-start.19 = (bf16[448,256]{1,0:T(8,128)(2,1)S(1)}, bf16[448,256]{1,0:T(8,128)(2,1)S(1)}, u32[]{:S(2)}, u32[]{:S(2)}) collective-permute-start(bf16[448,256]{1,0:T(8,128)(2,1)S(1)} %slice_bitcast_fusion), channel_id=1, source_target_pairs={{0,16},{16,0},{32,48},{48,32},{64,80},{80,64},{96,112},{112,96},{1... | collective-permute-start | bytes 688136 | tf_op jit(solution)/shard_map/ppermute | solution.py:10
  747.4 94.3 %copy-start.16 = (bf16[2,448,256]{2,1,0:T(8,128)(2,1)S(1)}, bf16[2,448,256]{2,1,0:T(8,128)(2,1)}, u32[]{:S(2)}) copy-start(bf16[2,448,256]{2,1,0:T(8,128)(2,1)} %reduce-scatter.8.cloned.1.call-done) | copy-start | bytes 1376260
  752.7 68.5 %collective-permute-start.17 = (bf16[448]{0:T(512)(128)(2,1)S(1)}, bf16[448]{0:T(512)(128)(2,1)S(1)}, u32[]{:S(2)}, u32[]{:S(2)}) collective-permute-start(bf16[448]{0:T(512)(128)(2,1)S(1)} %collective-permute-done.16), channel_id=1, source_target_pairs={{0,32},{16,48},{32,0},{48,16},{64,96},{80,112},{96,64},{112,80},{1... | collective-permute-start | bytes 2696 | tf_op jit(solution)/shard_map/ppermute | solution.py:10
  811.0 3.5 collective-permute-start.22
  814.6 3.5 collective-permute-start.23
  818.1 7.2 collective-permute-start.24
  821.1 5.1 collective-permute-start.18
  821.6 14.0 %collective-permute-start.27 = (bf16[256,448]{0,1:T(8,128)(2,1)S(1)}, bf16[256,448]{0,1:T(8,128)(2,1)S(1)}, u32[]{:S(2)}, u32[]{:S(2)}) collective-permute-start(bf16[256,448]{0,1:T(8,128)(2,1)S(1)} %collective-permute-done.26), channel_id=1, source_target_pairs={{0,64},{16,80},{32,96},{48,112},{64,0},{80,16},{96,32},{112,48},{1... | collective-permute-start | bytes 688136 | tf_op jit(solution)/shard_map/ppermute | solution.py:10
  824.7 9.5 %collective-permute-start.20 = (bf16[448,256]{1,0:T(8,128)(2,1)S(1)}, bf16[448,256]{1,0:T(8,128)(2,1)S(1)}, u32[]{:S(2)}, u32[]{:S(2)}) collective-permute-start(bf16[448,256]{1,0:T(8,128)(2,1)S(1)} %collective-permute-done.19), channel_id=1, source_target_pairs={{0,32},{16,48},{32,0},{48,16},{64,96},{80,112},{96,64},{112,80},{1... | collective-permute-start | bytes 688136 | tf_op jit(solution)/shard_map/ppermute | solution.py:10
  834.2 7.5 collective-permute-start.21
Sparse Core Ops, SparseCore 0:
  10.4 56.6 all-gather.6
  69.5 70.1 all-gather.8
  142.6 93.3 all-gather.10
  314.7 257.2 all-reduce.2
  575.8 71.7 reduce-scatter.9
  652.2 93.2 reduce-scatter.7
  749.6 60.3 reduce-scatter.11
